TPU v7x, 256 devices: a whole 4x4x8 slice. The times are simulated.
256 devices in a mesh: dp: 32 (over x, z), fsdp: 8 (over y, core).
Axes of the slice: x: 4, y: 4, z: 8, core: 2. Of those that a mesh axis runs over, the one named last changes fastest.
Arguments:
- hidden: bfloat16 [8192, 28672], P('dp', 'fsdp'), may hold values from -6 to 6
- cotangent: bfloat16 [8192, 8192], P('dp', 'fsdp'), may hold values from -6 to 6
- region_ids: int32 [8192], P('dp'), may hold values from 0 to 255, as said below
- adapter_a: bfloat16 [256, 64, 28672], P('dp', None, 'fsdp'), may hold values from -0.03125 to 0.03125
- adapter_b: bfloat16 [256, 64, 8192], P('dp', None, 'fsdp'), may hold values from -0.75 to 0.75
Outputs:
- grad_a: bfloat16 [256, 64, 28672], P('dp', None, 'fsdp')
- grad_b: bfloat16 [256, 64, 8192], P('dp', None, 'fsdp')
- grad_hidden: bfloat16 [8192, 28672], P('dp', 'fsdp')
Inputs may be any that keep to these rules, and one draw needn't show every extreme that they name: `region_ids`: region r belongs to owner r // 8. In each aligned block of 256 tokens (the tokens of one index of dp) the ids never fall, and at most 24 tokens name regions of one owner; in every block 4 owners, the same ones in every block, reach that bound.
All inputs are finite; a program needn't handle non-finite values.
Results may differ from a plain program's by a relative error of at most 0.0049.
Values may be sent and summed in bfloat16 or wider, within the bound.
A program may use at most 128 MiB of HBM per device.

v0:
```python
import jax
import jax.numpy as jnp
from jax import lax
from jax.sharding import PartitionSpec as P


def contract_rows(left, right):
    return lax.dot_general(
        left, right, (((0,), (0,)), ((), ())), preferred_element_type=jnp.float32
    )


def contract_cols(left, right):
    return lax.dot_general(
        left, right, (((1,), (1,)), ((), ())), preferred_element_type=jnp.float32
    )


def shards(hidden, cotangent, region_ids, adapter_a, adapter_b):
    owner_count = lax.axis_size("dp")
    token_count = hidden.shape[0]
    local_count = adapter_a.shape[0]
    rank_width = adapter_a.shape[1]
    hidden_width = hidden.shape[1]
    model_width = cotangent.shape[1]
    capacity = 3 * token_count // owner_count
    owner_of = region_ids // local_count
    owner_ids = jnp.arange(owner_count, dtype=jnp.int32)
    counts = jnp.sum((owner_of[:, None] == owner_ids[None, :]).astype(jnp.int32), axis=0)
    starts = jnp.cumsum(counts) - counts
    slot_index = jnp.arange(capacity, dtype=jnp.int32)
    usable = slot_index[None, :] < counts[:, None]
    row_index = jnp.where(usable, starts[:, None] + slot_index[None, :], token_count)
    id_width = 128
    table = jnp.concatenate(
        [
            hidden,
            cotangent,
            jnp.broadcast_to(
                (region_ids % local_count).astype(jnp.bfloat16)[:, None], (token_count, id_width)
            ),
        ],
        axis=-1,
    )
    flat_a = adapter_a.reshape(local_count * rank_width, hidden_width)
    flat_b = adapter_b.reshape(local_count * rank_width, model_width)
    local_ids = jnp.arange(local_count).astype(jnp.bfloat16)
    pieces = 2
    piece = capacity // pieces
    grad_a = None
    grad_b = None
    arrived = []
    for k in range(pieces):
        send = table.at[row_index[:, k * piece : (k + 1) * piece]].get(
            mode="fill", fill_value=local_count
        )
        recv = lax.all_to_all(send, "dp", split_axis=0, concat_axis=0, tiled=True)
        if k > 0:
            recv, full = lax.optimization_barrier((recv, full))
        rows = owner_count * piece
        recv = recv.reshape(rows, hidden_width + model_width + id_width)
        got_hidden = recv[:, :hidden_width]
        got_cotangent = recv[:, hidden_width : hidden_width + model_width]
        got_local = recv[:, hidden_width + model_width]
        onehot = (got_local[:, None] == local_ids[None, :]).astype(jnp.float32)
        part_down = contract_cols(got_hidden, flat_a).reshape(rows, local_count, rank_width)
        part_back = contract_cols(got_cotangent, flat_b).reshape(rows, local_count, rank_width)
        pick_down = jnp.sum(part_down * onehot[:, :, None], axis=1)
        pick_back = jnp.sum(part_back * onehot[:, :, None], axis=1)
        full = lax.psum(jnp.concatenate([pick_down, pick_back], axis=1), "fsdp")
        full_down = full[:, :rank_width].astype(jnp.bfloat16)
        full_back = full[:, rank_width:].astype(jnp.bfloat16)
        mask = onehot.astype(jnp.bfloat16)[:, :, None]
        down_rows = (mask * full_down[:, None, :]).reshape(rows, local_count * rank_width)
        back_rows = (mask * full_back[:, None, :]).reshape(rows, local_count * rank_width)
        returned = jnp.dot(back_rows, flat_a, preferred_element_type=jnp.float32).astype(
            jnp.bfloat16
        )
        returned = returned.reshape(owner_count, piece, hidden_width)
        arrived.append(lax.all_to_all(returned, "dp", split_axis=0, concat_axis=0, tiled=True))
        part_b = contract_rows(down_rows, got_cotangent)
        part_a = contract_rows(back_rows, got_hidden)
        grad_b = part_b if grad_b is None else grad_b + part_b
        grad_a = part_a if grad_a is None else grad_a + part_a
    grad_b = grad_b.reshape(local_count, rank_width, model_width).astype(jnp.bfloat16)
    grad_a = grad_a.reshape(local_count, rank_width, hidden_width).astype(jnp.bfloat16)
    arrived = jnp.concatenate(arrived, axis=1)
    before = jnp.sum((owner_of[None, :] < owner_of[:, None]).astype(jnp.int32), axis=1)
    position = jnp.arange(token_count, dtype=jnp.int32) - before
    grad_hidden = arrived.reshape(owner_count * capacity, hidden_width)[
        owner_of * capacity + position
    ]
    return (grad_a, grad_b, grad_hidden)


def solution(mesh):
    return jax.shard_map(
        shards,
        mesh=mesh,
        in_specs=(
            P("dp", "fsdp"),
            P("dp", "fsdp"),
            P("dp"),
            P("dp", None, "fsdp"),
            P("dp", None, "fsdp"),
        ),
        out_specs=(P("dp", None, "fsdp"), P("dp", None, "fsdp"), P("dp", "fsdp")),
        check_vma=False,
    )
```

profile of v0, /device:TPU:24, one launch (start us, length us, event | category | flops | bytes accessed | tf_op | source)
XLA Modules:
  0.0 509.1 jit_solution(9303705913638020247)
XLA Ops:
  0.6 0.0 copy-start
  0.6 0.8 and_select_fusion.1
  1.4 0.1 convert_reduce_fusion.1
  1.5 0.1 copy.10
  1.6 0.1 reduce-window.8
  1.7 0.1 reduce
  1.8 0.1 add_select_fusion
  1.9 0.1 compare_select_fusion
  2.0 0.1 compare_and_fusion
  2.1 0.1 reshape.230
  2.2 0.1 broadcast_in_dim.18
  2.3 1.8 pad_maximum_fusion.1
  4.1 4.6 gather_fusion
  8.7 6.8 %reshape.229 = bf16[32,12,4736]{2,1,0:T(8,128)(2,1)} reshape(bf16[384,4736]{1,0:T(8,128)(2,1)} %gather_fusion) | data formatting | bytes 7274496 | tf_op jit(solution)/shard_map/gather | solution.py:54
  15.5 5.2 %broadcast_select_fusion.1 = bf16[32,12,4736]{2,1,0:T(8,128)(2,1)} fusion(bf16[32,12,4736]{2,1,0:T(8,128)(2,1)} %reshape.229, pred[32,12]{1,0:T(8,128)(4,1)S(1)} %get-tuple-element.10), kind=kLoop, calls=%fused_computation.10 | loop fusion | flops 1818624 | bytes 7274880 | tf_op jit(solution)/shard_map/select_n | solution.py:54
  20.6 11.4 %all-to-all-start = ((bf16[32,12,4736]{2,1,0:T(8,128)(2,1)}), bf16[32,12,4736]{2,1,0:T(8,128)(2,1)}, u32[]{:S(2)}, u32[]{:S(2)}) async-start(bf16[32,12,4736]{2,1,0:T(8,128)(2,1)} %broadcast_select_fusion.1), calls=%async_computation | async-start | bytes 9699328 | tf_op jit(solution)/shard_map/all_to_all | solution.py:57
  32.1 0.1 reshape.238
  32.2 4.6 gather_fusion.1
  36.8 6.8 %reshape.237 = bf16[32,12,4736]{2,1,0:T(8,128)(2,1)} reshape(bf16[384,4736]{1,0:T(8,128)(2,1)} %gather_fusion.1) | data formatting | bytes 7274496 | tf_op jit(solution)/shard_map/gather | solution.py:54
  43.5 5.2 %broadcast_select_fusion = bf16[32,12,4736]{2,1,0:T(8,128)(2,1)} fusion(bf16[32,12,4736]{2,1,0:T(8,128)(2,1)} %reshape.237, pred[32,12]{1,0:T(8,128)(4,1)S(1)} %get-tuple-element.9), kind=kLoop, calls=%fused_computation.9 | loop fusion | flops 1818624 | bytes 7274880 | tf_op jit(solution)/shard_map/select_n | solution.py:54
  48.8 92.7 %all-to-all-done = bf16[32,12,4736]{2,1,0:T(8,128)(2,1)} async-done(((bf16[32,12,4736]{2,1,0:T(8,128)(2,1)}), bf16[32,12,4736]{2,1,0:T(8,128)(2,1)}, u32[]{:S(2)}, u32[]{:S(2)}) %all-to-all-start) | async-done | bytes 3637280 | tf_op jit(solution)/shard_map/all_to_all | solution.py:57
  141.5 7.7 %all-to-all-start.1 = ((bf16[32,12,4736]{2,1,0:T(8,128)(2,1)}), bf16[32,12,4736]{2,1,0:T(8,128)(2,1)}, u32[]{:S(2)}, u32[]{:S(2)}) async-start(bf16[32,12,4736]{2,1,0:T(8,128)(2,1)} %broadcast_select_fusion), calls=%async_computation.1 | async-start | bytes 9699328 | tf_op jit(solution)/shard_map/all_to_all | solution.py:57
  149.2 6.9 %reshape.223 = bf16[384,4736]{1,0:T(8,128)(2,1)} reshape(bf16[32,12,4736]{2,1,0:T(8,128)(2,1)} %all-to-all-done) | data formatting | bytes 7274496 | tf_op jit(solution)/shard_map/reshape | solution.py:61
  156.1 0.0 copy-start.1
  156.1 1.2 slice_reduce_fusion.1
  157.2 0.1 fusion.32
  157.3 0.0 copy-done
  157.3 1.9 fusion.17
  159.2 0.0 copy-done.1
  159.2 3.9 fusion.22
  163.1 25.8 %all-reduce.2 = bf16[384,128]{0,1:T(8,128)(2,1)S(1)} all-reduce(f32[384,128]{0,1:T(8,128)S(1)} %pad_maximum_fusion.2), channel_id=1, replica_groups=mesh['dp'=32,'fsdp'=8] {'fsdp'}, use_global_device_ids=true, to_apply=%region_4.5 | all-reduce | flops 49152 | bytes 294912 | tf_op jit(solution)/shard_map/psum | solution.py:70
  188.9 69.3 %all-to-all-done.1 = bf16[32,12,4736]{2,1,0:T(8,128)(2,1)} async-done(((bf16[32,12,4736]{2,1,0:T(8,128)(2,1)}), bf16[32,12,4736]{2,1,0:T(8,128)(2,1)}, u32[]{:S(2)}, u32[]{:S(2)}) %all-to-all-start.1) | async-done | bytes 3637280 | tf_op jit(solution)/shard_map/all_to_all | solution.py:57
  258.2 6.9 %reshape.224 = bf16[384,4736]{1,0:T(8,128)(2,1)} reshape(bf16[32,12,4736]{2,1,0:T(8,128)(2,1)} %all-to-all-done.1) | data formatting | bytes 7274496 | tf_op jit(solution)/shard_map/reshape | solution.py:61
  265.1 1.0 slice_reduce_fusion
  266.1 0.1 fusion.33
  266.2 5.0 fusion.19
  271.1 1.9 fusion.18
  273.0 22.5 %all-reduce.3 = bf16[384,128]{0,1:T(8,128)(2,1)S(1)} all-reduce(f32[384,128]{0,1:T(8,128)S(1)} %pad_maximum_fusion.3), channel_id=1, replica_groups=mesh['dp'=32,'fsdp'=8] {'fsdp'}, use_global_device_ids=true, to_apply=%region_7.8 | all-reduce | flops 49152 | bytes 294912 | tf_op jit(solution)/shard_map/psum | solution.py:70
  295.5 5.2 %fusion.1 = bf16[384,3584]{1,0:T(8,128)(2,1)} fusion(bf16[8,64,3584]{2,1,0:T(8,128)(2,1)} %param.8, bf16[384,64]{0,1:T(8,128)(2,1)S(1)} %get-tuple-element.6, bf16[384,8]{0,1:T(8,128)(2,1)S(1)} %get-tuple-element.17), kind=kOutput, calls=%fused_computation.7 | convolution fusion | flops 1410859008 | bytes 6477824 | tf_op jit(solution)/shard_map/dot_general | solution.py:76
  300.8 5.3 %reshape.226 = bf16[32,12,3584]{2,1,0:T(8,128)(2,1)} reshape(bf16[384,3584]{1,0:T(8,128)(2,1)} %fusion.1) | data formatting | bytes 5505024 | tf_op jit(solution)/shard_map/reshape | solution.py:79
  306.0 10.0 %all-to-all-start.3 = ((bf16[32,12,3584]{2,1,0:T(8,128)(2,1)}), bf16[32,12,3584]{2,1,0:T(8,128)(2,1)}, u32[]{:S(2)}, u32[]{:S(2)}) async-start(bf16[32,12,3584]{2,1,0:T(8,128)(2,1)} %reshape.226), calls=%async_computation.3 | async-start | bytes 7340032 | tf_op jit(solution)/shard_map/all_to_all | solution.py:80
  316.0 5.2 %fusion = bf16[384,3584]{1,0:T(8,128)(2,1)} fusion(bf16[8,64,3584]{2,1,0:T(8,128)(2,1)} %param.8, bf16[384,64]{0,1:T(8,128)(2,1)S(1)} %get-tuple-element.8, bf16[384,8]{0,1:T(8,128)(2,1)S(1)} %get-tuple-element.19), kind=kOutput, calls=%fused_computation.6 | convolution fusion | flops 1410859008 | bytes 6477824 | tf_op jit(solution)/shard_map/dot_general | solution.py:76
  321.2 5.3 %reshape.225 = bf16[32,12,3584]{2,1,0:T(8,128)(2,1)} reshape(bf16[384,3584]{1,0:T(8,128)(2,1)} %fusion) | data formatting | bytes 5505024 | tf_op jit(solution)/shard_map/reshape | solution.py:79
  326.5 74.0 %all-to-all-done.3 = bf16[32,12,3584]{2,1,0:T(8,128)(2,1)} async-done(((bf16[32,12,3584]{2,1,0:T(8,128)(2,1)}), bf16[32,12,3584]{2,1,0:T(8,128)(2,1)}, u32[]{:S(2)}, u32[]{:S(2)}) %all-to-all-start.3) | async-done | bytes 2752544 | tf_op jit(solution)/shard_map/all_to_all | solution.py:80
  400.5 7.4 %all-to-all-start.2 = ((bf16[32,12,3584]{2,1,0:T(8,128)(2,1)}), bf16[32,12,3584]{2,1,0:T(8,128)(2,1)}, u32[]{:S(2)}, u32[]{:S(2)}) async-start(bf16[32,12,3584]{2,1,0:T(8,128)(2,1)} %reshape.225), calls=%async_computation.2 | async-start | bytes 7340032 | tf_op jit(solution)/shard_map/all_to_all | solution.py:80
  407.9 0.0 copy-start.3
  407.9 0.2 convert_reduce_fusion
  408.1 0.1 broadcast_multiply_fusion
  408.2 0.1 broadcast_multiply_fusion.1
  408.3 0.0 copy-start.2
  408.3 2.0 fusion.29
  410.4 0.0 copy-done.3
  410.4 1.7 add_convert_fusion.1
  412.1 0.0 copy-done.2
  412.1 2.1 fusion.8
  414.1 3.9 add_convert_fusion
  418.1 75.9 %all-to-all-done.2 = bf16[32,12,3584]{2,1,0:T(8,128)(2,1)} async-done(((bf16[32,12,3584]{2,1,0:T(8,128)(2,1)}), bf16[32,12,3584]{2,1,0:T(8,128)(2,1)}, u32[]{:S(2)}, u32[]{:S(2)}) %all-to-all-start.2) | async-done | bytes 2752544 | tf_op jit(solution)/shard_map/all_to_all | solution.py:80
  493.9 7.1 %pad_maximum_fusion = bf16[32,24,3584]{2,1,0:T(8,128)(2,1)} fusion(bf16[32,12,3584]{2,1,0:T(8,128)(2,1)} %all-to-all-done.3, bf16[32,12,3584]{2,1,0:T(8,128)(2,1)} %all-to-all-done.2), kind=kLoop, calls=%fused_computation.8 | loop fusion | flops 11010048 | bytes 11010048 | tf_op jit(solution)/shard_map/concatenate | solution.py:87
  501.0 8.0 %gather_fusion.2 = bf16[256,3584]{1,0:T(8,128)(2,1)} fusion(bf16[768,3584]{1,0:T(8,128)(2,1)} %bitcast.46, s32[1024]{0:T(1024)S(1)} %pad_clamp_fusion), kind=kCustom, calls=%fused_computation.2 | custom fusion | bytes 3671040 | tf_op jit(solution)/shard_map/gather | solution.py:90
  (10 shorter events, 0.1 us)
Async XLA Ops:
  0.6 156.7 %copy-start = (bf16[8,64,1024]{2,1,0:T(8,128)(2,1)S(1)}, bf16[8,64,1024]{2,1,0:T(8,128)(2,1)}, u32[]{:S(2)}) copy-start(bf16[8,64,1024]{2,1,0:T(8,128)(2,1)} %param.9) | copy-start | bytes 3145732
  20.6 120.8 %all-to-all-start = ((bf16[32,12,4736]{2,1,0:T(8,128)(2,1)}), bf16[32,12,4736]{2,1,0:T(8,128)(2,1)}, u32[]{:S(2)}, u32[]{:S(2)}) async-start(bf16[32,12,4736]{2,1,0:T(8,128)(2,1)} %broadcast_select_fusion.1), calls=%async_computation | async-start | bytes 9699328 | tf_op jit(solution)/shard_map/all_to_all | solution.py:57
  141.5 116.8 %all-to-all-start.1 = ((bf16[32,12,4736]{2,1,0:T(8,128)(2,1)}), bf16[32,12,4736]{2,1,0:T(8,128)(2,1)}, u32[]{:S(2)}, u32[]{:S(2)}) async-start(bf16[32,12,4736]{2,1,0:T(8,128)(2,1)} %broadcast_select_fusion), calls=%async_computation.1 | async-start | bytes 9699328 | tf_op jit(solution)/shard_map/all_to_all | solution.py:57
  156.1 3.1 copy-start.1
  306.0 94.5 %all-to-all-start.3 = ((bf16[32,12,3584]{2,1,0:T(8,128)(2,1)}), bf16[32,12,3584]{2,1,0:T(8,128)(2,1)}, u32[]{:S(2)}, u32[]{:S(2)}) async-start(bf16[32,12,3584]{2,1,0:T(8,128)(2,1)} %reshape.226), calls=%async_computation.3 | async-start | bytes 7340032 | tf_op jit(solution)/shard_map/all_to_all | solution.py:80
  400.5 93.4 %all-to-all-start.2 = ((bf16[32,12,3584]{2,1,0:T(8,128)(2,1)}), bf16[32,12,3584]{2,1,0:T(8,128)(2,1)}, u32[]{:S(2)}, u32[]{:S(2)}) async-start(bf16[32,12,3584]{2,1,0:T(8,128)(2,1)} %reshape.225), calls=%async_computation.2 | async-start | bytes 7340032 | tf_op jit(solution)/shard_map/all_to_all | solution.py:80
  407.9 2.5 copy-start.3
  408.3 3.8 copy-start.2
where the time goes:
time: 511 us; the launch traced here: 509 us
  waiting for transfers between devices  312 us (61%)
  local copies, waits for them, and re-layouts  57.6 us (11%)
  blocking collectives  48.2 us (9%)
  starting transfers between devices  36.5 us (7%)
  matrix products  32.7 us (6%)
  other arithmetic  21.2 us (4%)
    all_to_all x2, waiting for transfers between devices, shards(): recv = lax.all_to_all(send, 'dp', split_axis=0, concat_axis=0, tiled=True)  162 us
    all_to_all x2, waiting for transfers between devices, shards(): lax.all_to_all(returned, 'dp', split_axis=0, concat_axis=0, tiled=True)  150 us
    psum x2, blocking collectives, shards(): full = lax.psum(jnp.concatenate([pick_down, pick_back], axis=1), 'fsdp')  48.2 us
    gather x4, local copies, waits for them, and re-layouts, shards(): table.at[row_index[:, k * piece:(k + 1) * piece]]  22.7 us
    all_to_all x2, starting transfers between devices, shards(): recv = lax.all_to_all(send, 'dp', split_axis=0, concat_axis=0, tiled=True)  19.1 us
    all_to_all x2, starting transfers between devices, shards(): lax.all_to_all(returned, 'dp', split_axis=0, concat_axis=0, tiled=True)  17.4 us
    reshape x2, local copies, waits for them, and re-layouts, shards(): recv = recv.reshape(rows, hidden_width + model_width + id_width)  13.7 us
    dot_general x4, matrix products, contract_cols(): lax.dot_general(left, right, (((1,), (1,)), ((), ())), preferred_element_...  12.6 us
  transfers between devices with their start and end apart: 4, of which 4 were waited for; matrix products, arithmetic and copies ran while one was open for 10% of the time, Pallas kernels for 0%

commit v1 on v0

--- a/solution.py
+++ b/solution.py
@@ -67,7 +67,9 @@
         part_back = contract_cols(got_cotangent, flat_b).reshape(rows, local_count, rank_width)
         pick_down = jnp.sum(part_down * onehot[:, :, None], axis=1)
         pick_back = jnp.sum(part_back * onehot[:, :, None], axis=1)
-        full = lax.psum(jnp.concatenate([pick_down, pick_back], axis=1), "fsdp")
+        full = jnp.sum(
+            lax.all_gather(jnp.concatenate([pick_down, pick_back], axis=1), "fsdp"), axis=0
+        )
         full_down = full[:, :rank_width].astype(jnp.bfloat16)
         full_back = full[:, rank_width:].astype(jnp.bfloat16)
         mask = onehot.astype(jnp.bfloat16)[:, :, None]

time: 511 us -> 473 us (0.926)
  blocking collectives: 48.2 us -> 0 us
  between operations: 0.88 us -> 14.3 us
  matrix products: 32.7 us -> 27.5 us
    all_gather x0 -> x2, waiting for transfers between devices: none -> 52.9 us  [shards(): lax.all_gather(jnp.concatenate([pick_down, pick_back], axis=1), 'fsdp')]
    psum x2 -> x0, blocking collectives: 48.2 us -> none  [shards(): full = lax.psum(jnp.concatenate([pick_down, pick_back], axis=1), 'fsdp')]
    all_to_all x2, waiting for transfers between devices: 150 us -> 109 us  [shards(): lax.all_to_all(returned, 'dp', split_axis=0, concat_axis=0, tiled=True)]
    all_to_all x2, waiting for transfers between devices: 162 us -> 150 us  [shards(): recv = lax.all_to_all(send, 'dp', split_axis=0, concat_axis=0, tiled=True)]
  transfers between devices with their start and end apart: 4 -> 6, of which waited for: 4 -> 6; matrix products, arithmetic and copies ran while one was open for 10% -> 16% of each run, Pallas kernels for 0% -> 0%
where the time goes in v1:
time: 473 us; the launch traced here: 471 us
  waiting for transfers between devices  312 us (66%)
  local copies, waits for them, and re-layouts  61.9 us (13%)
  starting transfers between devices  32.8 us (7%)
  matrix products  27.5 us (6%)
  other arithmetic  23.3 us (5%)
  between operations  14.3 us (3%)
    all_to_all x2, waiting for transfers between devices, shards(): recv = lax.all_to_all(send, 'dp', split_axis=0, concat_axis=0, tiled=True)  150 us
    all_to_all x2, waiting for transfers between devices, shards(): lax.all_to_all(returned, 'dp', split_axis=0, concat_axis=0, tiled=True)  109 us
    all_gather x2, waiting for transfers between devices, shards(): lax.all_gather(jnp.concatenate([pick_down, pick_back], axis=1), 'fsdp')  52.9 us
    gather x4, local copies, waits for them, and re-layouts, shards(): table.at[row_index[:, k * piece:(k + 1) * piece]]  22.7 us
    all_to_all x2, starting transfers between devices, shards(): recv = lax.all_to_all(send, 'dp', split_axis=0, concat_axis=0, tiled=True)  19.1 us
    reshape x2, local copies, waits for them, and re-layouts, shards(): recv = recv.reshape(rows, hidden_width + model_width + id_width)  13.7 us
    all_to_all x2, starting transfers between devices, shards(): lax.all_to_all(returned, 'dp', split_axis=0, concat_axis=0, tiled=True)  13.4 us
    dot_general x4, matrix products, contract_cols(): lax.dot_general(left, right, (((1,), (1,)), ((), ())), preferred_element_...  11.5 us
  transfers between devices with their start and end apart: 6, of which 6 were waited for; matrix products, arithmetic and copies ran while one was open for 16% of the time, Pallas kernels for 0%

profile of v1, /device:TPU:24, one launch (start us, length us, event | category | flops | bytes accessed | tf_op | source)
XLA Modules:
  0.0 471.4 jit_solution(16651891020978609080)
XLA Ops:
  7.2 0.0 copy-start
  7.2 0.8 and_select_fusion.1
  8.0 0.1 convert_reduce_fusion.1
  8.1 0.1 copy.11
  8.2 0.1 reduce-window.8
  8.2 0.1 reduce
  8.3 0.1 add_select_fusion
  8.4 0.1 compare_select_fusion
  8.5 0.1 compare_and_fusion
  8.6 0.1 reshape.230
  8.7 0.1 broadcast_in_dim.18
  8.8 1.8 pad_maximum_fusion.1
  10.7 4.6 gather_fusion
  15.2 6.8 %reshape.229 = bf16[32,12,4736]{2,1,0:T(8,128)(2,1)} reshape(bf16[384,4736]{1,0:T(8,128)(2,1)} %gather_fusion) | data formatting | bytes 7274496 | tf_op jit(solution)/shard_map/gather | solution.py:54
  22.0 5.2 %broadcast_select_fusion.1 = bf16[32,12,4736]{2,1,0:T(8,128)(2,1)} fusion(bf16[32,12,4736]{2,1,0:T(8,128)(2,1)} %reshape.229, pred[32,12]{1,0:T(8,128)(4,1)S(1)} %get-tuple-element.10), kind=kLoop, calls=%fused_computation.10 | loop fusion | flops 1818624 | bytes 7274880 | tf_op jit(solution)/shard_map/select_n | solution.py:54
  27.2 11.4 %all-to-all-start = ((bf16[32,12,4736]{2,1,0:T(8,128)(2,1)}), bf16[32,12,4736]{2,1,0:T(8,128)(2,1)}, u32[]{:S(2)}, u32[]{:S(2)}) async-start(bf16[32,12,4736]{2,1,0:T(8,128)(2,1)} %broadcast_select_fusion.1), calls=%async_computation | async-start | bytes 9699328 | tf_op jit(solution)/shard_map/all_to_all | solution.py:57
  38.6 0.1 reshape.238
  38.7 4.6 gather_fusion.1
  43.3 6.8 %reshape.237 = bf16[32,12,4736]{2,1,0:T(8,128)(2,1)} reshape(bf16[384,4736]{1,0:T(8,128)(2,1)} %gather_fusion.1) | data formatting | bytes 7274496 | tf_op jit(solution)/shard_map/gather | solution.py:54
  50.1 5.1 %broadcast_select_fusion = bf16[32,12,4736]{2,1,0:T(8,128)(2,1)} fusion(bf16[32,12,4736]{2,1,0:T(8,128)(2,1)} %reshape.237, pred[32,12]{1,0:T(8,128)(4,1)S(1)} %get-tuple-element.9), kind=kLoop, calls=%fused_computation.9 | loop fusion | flops 1818624 | bytes 7274880 | tf_op jit(solution)/shard_map/select_n | solution.py:54
  55.2 92.8 %all-to-all-done = bf16[32,12,4736]{2,1,0:T(8,128)(2,1)} async-done(((bf16[32,12,4736]{2,1,0:T(8,128)(2,1)}), bf16[32,12,4736]{2,1,0:T(8,128)(2,1)}, u32[]{:S(2)}, u32[]{:S(2)}) %all-to-all-start) | async-done | bytes 3637280 | tf_op jit(solution)/shard_map/all_to_all | solution.py:57
  148.0 7.7 %all-to-all-start.1 = ((bf16[32,12,4736]{2,1,0:T(8,128)(2,1)}), bf16[32,12,4736]{2,1,0:T(8,128)(2,1)}, u32[]{:S(2)}, u32[]{:S(2)}) async-start(bf16[32,12,4736]{2,1,0:T(8,128)(2,1)} %broadcast_select_fusion), calls=%async_computation.1 | async-start | bytes 9699328 | tf_op jit(solution)/shard_map/all_to_all | solution.py:57
  155.7 0.0 all-gather.5.cloned.1.call-start
  155.8 6.9 %reshape.223 = bf16[384,4736]{1,0:T(8,128)(2,1)} reshape(bf16[32,12,4736]{2,1,0:T(8,128)(2,1)} %all-to-all-done) | data formatting | bytes 7274496 | tf_op jit(solution)/shard_map/reshape | solution.py:61
  162.6 1.2 slice_reduce_fusion.1
  163.8 0.1 fusion.32
  163.9 1.9 fusion.17
  165.8 3.9 fusion.22
  169.6 0.7 pad_maximum_fusion.2
  170.3 0.0 all-gather.5.cloned.1.call-update
  170.3 26.5 %all-gather.5.cloned.1.call-done = f32[3072,128]{0,1:T(8,128)} async-done(((f32[384,128]{0,1:T(8,128)}), f32[3072,128]{0,1:T(8,128)}) %all-gather.5.cloned.1.call-update) | async-done | bytes 1572880 | tf_op jit(solution)/shard_map/all_gather | solution.py:71
  196.8 1.8 copy.12
  198.7 0.4 bitcast_reduce_fusion.1
  199.1 0.2 copy-done.2
  199.3 3.2 fusion
  202.5 5.3 %reshape.225 = bf16[32,12,3584]{2,1,0:T(8,128)(2,1)} reshape(bf16[384,3584]{1,0:T(8,128)(2,1)} %fusion) | data formatting | bytes 5505024 | tf_op jit(solution)/shard_map/reshape | solution.py:81
  207.7 57.0 %all-to-all-done.1 = bf16[32,12,4736]{2,1,0:T(8,128)(2,1)} async-done(((bf16[32,12,4736]{2,1,0:T(8,128)(2,1)}), bf16[32,12,4736]{2,1,0:T(8,128)(2,1)}, u32[]{:S(2)}, u32[]{:S(2)}) %all-to-all-start.1) | async-done | bytes 3637280 | tf_op jit(solution)/shard_map/all_to_all | solution.py:57
  264.8 7.9 %all-to-all-start.2 = ((bf16[32,12,3584]{2,1,0:T(8,128)(2,1)}), bf16[32,12,3584]{2,1,0:T(8,128)(2,1)}, u32[]{:S(2)}, u32[]{:S(2)}) async-start(bf16[32,12,3584]{2,1,0:T(8,128)(2,1)} %reshape.225), calls=%async_computation.2 | async-start | bytes 7340032 | tf_op jit(solution)/shard_map/all_to_all | solution.py:82
  272.7 0.2 all-gather.7.cloned.1.call-start
  272.9 6.9 %reshape.224 = bf16[384,4736]{1,0:T(8,128)(2,1)} reshape(bf16[32,12,4736]{2,1,0:T(8,128)(2,1)} %all-to-all-done.1) | data formatting | bytes 7274496 | tf_op jit(solution)/shard_map/reshape | solution.py:61
  279.8 1.2 slice_reduce_fusion
  280.9 0.1 fusion.33
  281.0 1.9 fusion.18
  282.9 3.9 fusion.19
  286.8 0.7 pad_maximum_fusion.3
  287.5 0.0 all-gather.7.cloned.1.call-update
  287.5 26.5 %all-gather.7.cloned.1.call-done = f32[3072,128]{0,1:T(8,128)} async-done(((f32[384,128]{0,1:T(8,128)}), f32[3072,128]{0,1:T(8,128)}) %all-gather.7.cloned.1.call-update) | async-done | bytes 1572880 | tf_op jit(solution)/shard_map/all_gather | solution.py:71
  313.9 1.8 copy.13
  315.8 0.4 bitcast_reduce_fusion
  316.2 0.2 copy-done.4
  316.5 3.2 fusion.1
  319.7 5.3 %reshape.226 = bf16[32,12,3584]{2,1,0:T(8,128)(2,1)} reshape(bf16[384,3584]{1,0:T(8,128)(2,1)} %fusion.1) | data formatting | bytes 5505024 | tf_op jit(solution)/shard_map/reshape | solution.py:81
  325.0 33.4 %all-to-all-done.2 = bf16[32,12,3584]{2,1,0:T(8,128)(2,1)} async-done(((bf16[32,12,3584]{2,1,0:T(8,128)(2,1)}), bf16[32,12,3584]{2,1,0:T(8,128)(2,1)}, u32[]{:S(2)}, u32[]{:S(2)}) %all-to-all-start.2) | async-done | bytes 2752544 | tf_op jit(solution)/shard_map/all_to_all | solution.py:82
  358.4 5.5 %all-to-all-start.3 = ((bf16[32,12,3584]{2,1,0:T(8,128)(2,1)}), bf16[32,12,3584]{2,1,0:T(8,128)(2,1)}, u32[]{:S(2)}, u32[]{:S(2)}) async-start(bf16[32,12,3584]{2,1,0:T(8,128)(2,1)} %reshape.226), calls=%async_computation.3 | async-start | bytes 7340032 | tf_op jit(solution)/shard_map/all_to_all | solution.py:82
  364.0 0.2 convert_reduce_fusion
  364.2 0.1 broadcast_multiply_fusion.1
  364.3 2.0 fusion.29
  366.3 2.1 fusion.8
  368.4 0.1 broadcast_multiply_fusion
  368.5 1.7 add_convert_fusion.1
  370.2 3.9 add_convert_fusion
  374.1 75.5 %all-to-all-done.3 = bf16[32,12,3584]{2,1,0:T(8,128)(2,1)} async-done(((bf16[32,12,3584]{2,1,0:T(8,128)(2,1)}), bf16[32,12,3584]{2,1,0:T(8,128)(2,1)}, u32[]{:S(2)}, u32[]{:S(2)}) %all-to-all-start.3) | async-done | bytes 2752544 | tf_op jit(solution)/shard_map/all_to_all | solution.py:82
  449.5 7.0 %pad_maximum_fusion = bf16[32,24,3584]{2,1,0:T(8,128)(2,1)} fusion(bf16[32,12,3584]{2,1,0:T(8,128)(2,1)} %all-to-all-done.3, bf16[32,12,3584]{2,1,0:T(8,128)(2,1)} %all-to-all-done.2), kind=kLoop, calls=%fused_computation.8 | loop fusion | flops 11010048 | bytes 11010048 | tf_op jit(solution)/shard_map/concatenate | solution.py:89
  456.6 8.0 %gather_fusion.2 = bf16[256,3584]{1,0:T(8,128)(2,1)} fusion(bf16[768,3584]{1,0:T(8,128)(2,1)} %bitcast.56, s32[1024]{0:T(1024)S(1)} %pad_clamp_fusion), kind=kCustom, calls=%fused_computation.2 | custom fusion | bytes 3671040 | tf_op jit(solution)/shard_map/gather | solution.py:92
  (19 shorter events, 0.1 us)
Async XLA Ops:
  7.2 156.7 %copy-start = (bf16[8,64,1024]{2,1,0:T(8,128)(2,1)S(1)}, bf16[8,64,1024]{2,1,0:T(8,128)(2,1)}, u32[]{:S(2)}) copy-start(bf16[8,64,1024]{2,1,0:T(8,128)(2,1)} %param.9) | copy-start | bytes 3145732
  27.2 120.8 %all-to-all-start = ((bf16[32,12,4736]{2,1,0:T(8,128)(2,1)}), bf16[32,12,4736]{2,1,0:T(8,128)(2,1)}, u32[]{:S(2)}, u32[]{:S(2)}) async-start(bf16[32,12,4736]{2,1,0:T(8,128)(2,1)} %broadcast_select_fusion.1), calls=%async_computation | async-start | bytes 9699328 | tf_op jit(solution)/shard_map/all_to_all | solution.py:57
  148.0 116.8 %all-to-all-start.1 = ((bf16[32,12,4736]{2,1,0:T(8,128)(2,1)}), bf16[32,12,4736]{2,1,0:T(8,128)(2,1)}, u32[]{:S(2)}, u32[]{:S(2)}) async-start(bf16[32,12,4736]{2,1,0:T(8,128)(2,1)} %broadcast_select_fusion), calls=%async_computation.1 | async-start | bytes 9699328 | tf_op jit(solution)/shard_map/all_to_all | solution.py:57
  155.7 41.1 %all-gather.5.cloned.1.call-start = ((), (), s32[]{:S(2)}) async-start(), calls=%async_computation.4 | async-start | bytes 1769472 | tf_op jit(solution)/shard_map/all_gather | solution.py:71
  162.6 3.1 copy-start.1
  196.8 2.5 copy-start.2
  264.8 93.6 %all-to-all-start.2 = ((bf16[32,12,3584]{2,1,0:T(8,128)(2,1)}), bf16[32,12,3584]{2,1,0:T(8,128)(2,1)}, u32[]{:S(2)}, u32[]{:S(2)}) async-start(bf16[32,12,3584]{2,1,0:T(8,128)(2,1)} %reshape.225), calls=%async_computation.2 | async-start | bytes 7340032 | tf_op jit(solution)/shard_map/all_to_all | solution.py:82
  272.7 41.3 %all-gather.7.cloned.1.call-start = ((), (), s32[]{:S(2)}) async-start(), calls=%async_computation.5 | async-start | bytes 1769472 | tf_op jit(solution)/shard_map/all_gather | solution.py:71
  279.8 3.1 copy-start.3
  313.9 2.5 copy-start.4
  358.4 91.1 %all-to-all-start.3 = ((bf16[32,12,3584]{2,1,0:T(8,128)(2,1)}), bf16[32,12,3584]{2,1,0:T(8,128)(2,1)}, u32[]{:S(2)}, u32[]{:S(2)}) async-start(bf16[32,12,3584]{2,1,0:T(8,128)(2,1)} %reshape.226), calls=%async_computation.3 | async-start | bytes 7340032 | tf_op jit(solution)/shard_map/all_to_all | solution.py:82
  364.0 2.3 copy-start.5
  366.3 2.2 copy-start.6
Sparse Core Ops, SparseCore 0:
  170.5 26.3 all-gather.4
  287.6 26.2 all-gather.6
